TPU v7x, 512 devices: a whole 4x4x16 slice. The times are simulated.
512 devices in a mesh: blk: 64 (over y_hi, z, core), fld: 8 (over x, y_lo).
Axes of the slice: x: 4, y: 4 (y_hi: 2, y_lo: 2; y = y_hi * 2 + y_lo), z: 16, core: 2. Of those that a mesh axis runs over, the one named last changes fastest.
Arguments:
- vectors: bfloat16 [4096, 16384], P('blk', 'fld'), may hold values from -1.1953125 to 1.1953125
- norms: bfloat16 [4096], P('blk'), may hold values from 0.5 to 2
- offsets: int32 [2], replicated, may hold values from 1 to 31
- pivot_block: int32 [2, 3], replicated, may hold values from 0 to 63
- pivot_row: int32 [2, 3], replicated, may hold values from 0 to 63
Outputs:
- similarity: bfloat16 [2, 3, 4096, 64], P(None, None, ('blk', 'fld'))
All inputs are finite; a program needn't handle non-finite values.
Results may differ from a plain program's by a relative error of at most 0.014.
Values may be sent and summed in bfloat16 or wider, within the bound.
No kernel may reach another device: no remote copies, remote signals or barrier semaphores. Data moves between devices by JAX's collectives and lax.ppermute only.
A program may use at most 64 MiB of HBM per device.

v0:
```python
import jax
import jax.numpy as jnp
from jax import lax
from jax.sharding import PartitionSpec as P

NOFF = 2


def from_behind(value, axis, by):
    peers = lax.axis_size(axis)
    return lax.ppermute(value, axis, [(i, (i + by) % peers) for i in range(peers)])


def from_root(value, axis, root):
    mine = lax.axis_index(axis) == root
    return lax.psum(jnp.where(mine, value, jnp.zeros_like(value)), axis)


def body(vectors, norms, offsets, pivot_block, pivot_row):
    rows = vectors.shape[0]
    blocks = lax.axis_size("blk")
    slices = lax.axis_size("fld")
    place = lax.axis_index("fld")
    share = rows // slices
    levels = (blocks // 2 - 1).bit_length()
    count_piv = pivot_block.shape[1]
    steps = NOFF * count_piv
    found_blocks = []
    found_norms = []
    for turn in range(NOFF):
        cur_block, cur_norm = (vectors, norms)
        for level in range(levels):
            moved = from_behind((cur_block, cur_norm), "blk", -(1 << level))
            taken = offsets[turn] // (1 << level) % 2 == 1
            cur_block = jnp.where(taken, moved[0], cur_block)
            cur_norm = jnp.where(taken, moved[1], cur_norm)
        found_blocks.append(cur_block)
        found_norms.append(cur_norm)
    partners = jnp.stack(found_blocks)
    partner_norms = jnp.stack(found_norms)
    flat_block = pivot_block.reshape(-1)
    flat_row = pivot_row.reshape(-1)

    def tile(step):
        turn = step // count_piv
        row = flat_row[step]
        candidate = lax.dynamic_index_in_dim(vectors, row, 0, keepdims=False)
        cand_norm = lax.dynamic_index_in_dim(norms, row, 0, keepdims=False)
        pivot, pivot_norm = (
            from_root(candidate, "blk", flat_block[step]),
            from_root(cand_norm, "blk", flat_block[step]),
        )
        pivot_norm = pivot_norm.astype(jnp.float32)
        partner = lax.dynamic_index_in_dim(partners, turn, 0, keepdims=False)
        scaled = (vectors.astype(jnp.float32) * pivot.astype(jnp.float32)[None, :]).astype(
            jnp.bfloat16
        )
        partial_value = lax.dot_general(
            scaled, partner, (((1,), (1,)), ((), ())), preferred_element_type=jnp.float32
        )
        return (partial_value.astype(jnp.bfloat16), pivot_norm)

    step_ids = jnp.arange(steps, dtype=jnp.int32)

    def step_each(carry, step):
        partial_value, pivot_norm = tile(step)
        summed_rows = lax.psum_scatter(
            partial_value, "fld", scatter_dimension=0, tiled=True
        ).astype(jnp.float32)
        return (carry, (summed_rows, pivot_norm))

    _, (field_sum, pivot_norms) = lax.scan(step_each, jnp.zeros((), jnp.float32), step_ids)
    own_norms = lax.dynamic_slice_in_dim(norms, place * share, share, 0).astype(jnp.float32)
    step_partner_norms = jnp.repeat(partner_norms.astype(jnp.float32), count_piv, axis=0)
    denominator = (
        own_norms[None, :, None] * pivot_norms[:, None, None] * step_partner_norms[:, None, :]
    )
    result = (field_sum / denominator).astype(jnp.bfloat16)
    return result.reshape(NOFF, count_piv, share, rows)


def solution(mesh):
    return jax.shard_map(
        body,
        mesh=mesh,
        in_specs=(P("blk", "fld"), P("blk"), P(), P(), P()),
        out_specs=P(None, None, ("blk", "fld"), None),
        check_vma=False,
    )
```

profile of v0, /device:TPU:16, one launch (start us, length us, event | category | flops | bytes accessed | tf_op | source)
XLA Modules:
  0.0 1268.1 jit_solution(18428325316396004109)
XLA Ops:
  0.0 10.7 collective-permute-start.9
  10.7 2.6 collective-permute-start
  13.3 1.4 fusion.7
  22.6 2.9 collective-permute-start.10
  25.5 2.9 collective-permute-start.14
  28.5 4.6 collective-permute-start.11
  33.1 3.4 collective-permute-start.15
  36.5 3.8 collective-permute-start.12
  40.3 2.9 collective-permute-start.16
  43.3 2.6 collective-permute-done.12
  45.8 10.3 collective-permute-start.13
  56.2 6.8 collective-permute-start.17
  63.2 10.5 collective-permute-start.1
  73.7 7.2 collective-permute-start.5
  81.0 1.9 collective-permute-start.2
  82.9 9.1 collective-permute-done.5
  92.0 1.9 collective-permute-start.6
  94.0 7.5 collective-permute-done.2
  101.5 10.9 collective-permute-start.3
  112.4 27.2 %collective-permute-done.6 = bf16[64,2048]{1,0:T(8,128)(2,1)S(1)} collective-permute-done((bf16[64,2048]{1,0:T(8,128)(2,1)S(1)}, bf16[64,2048]{1,0:T(8,128)(2,1)S(1)}, u32[]{:S(2)}, u32[]{:S(2)}) %collective-permute-start.6) | collective-permute-done | bytes 262176 | tf_op jit(solution)/shard_map/ppermute | solution.py:11
  139.6 23.4 %collective-permute-start.7 = (bf16[64,2048]{1,0:T(8,128)(2,1)S(1)}, bf16[64,2048]{1,0:T(8,128)(2,1)S(1)}, u32[]{:S(2)}, u32[]{:S(2)}) collective-permute-start(bf16[64,2048]{1,0:T(8,128)(2,1)S(1)} %broadcast_select_fusion.3), channel_id=1, source_target_pairs={{0,448},{8,456},{16,464},{24,472},{32,480},{40,488},{48,496},{56,5... | collective-permute-start | bytes 786440 | tf_op jit(solution)/shard_map/ppermute | solution.py:11
  163.1 17.4 %collective-permute-start.4 = (bf16[64,2048]{1,0:T(8,128)(2,1)S(1)}, bf16[64,2048]{1,0:T(8,128)(2,1)S(1)}, u32[]{:S(2)}, u32[]{:S(2)}) collective-permute-start(bf16[64,2048]{1,0:T(8,128)(2,1)S(1)} %broadcast_select_fusion.8), channel_id=1, source_target_pairs={{0,384},{8,392},{16,400},{24,408},{32,416},{40,424},{48,432},{56,4... | collective-permute-start | bytes 786440 | tf_op jit(solution)/shard_map/ppermute | solution.py:11
  180.5 12.0 collective-permute-done.7
  192.5 5.6 collective-permute-start.8
  198.1 14.0 %collective-permute-done.8 = bf16[64,2048]{1,0:T(8,128)(2,1)S(1)} collective-permute-done((bf16[64,2048]{1,0:T(8,128)(2,1)S(1)}, bf16[64,2048]{1,0:T(8,128)(2,1)S(1)}, u32[]{:S(2)}, u32[]{:S(2)}) %collective-permute-start.8) | collective-permute-done | bytes 262176 | tf_op jit(solution)/shard_map/ppermute | solution.py:11
  212.2 1055.1 %while.14 = (s32[]{:T(128)}, f32[6,8,64]{2,1,0:T(8,128)S(1)}, f32[6]{0:T(128)S(1)}, bf16[64,2048]{1,0:T(8,128)(2,1)S(1)}, s32[6]{0:T(128)S(1)}, /*index=5*/s32[6...) while((s32[]{:T(128)}, f32[6,8,64]{2,1,0:T(8,128)S(1)}, ...), condition=%wide.region_4.5_spmd, body=%wide.region_0.4_spmd.sunk | while | flops 17185304 | bytes 592440 | solution.py:72
  220.2 132.0 %all-reduce.4 = (bf16[2048]{0:T(1024)(128)(2,1)S(1)}, bf16[1]{0:T(256)(128)(2,1)}) all-reduce(bf16[2048]{0:T(1024)(128)(2,1)S(1)} %fusion.11, bf16[1]{0:T(256)(128)(2,1)} %bitcast.37), channel_id=1, replica_groups=mesh['blk'=64,'fld'=8] {'blk'}, use_global_device_ids=true, to_apply=%region_1.1 | all-reduce | flops 2049 | bytes 8196 | tf_op jit(solution)/shard_map/while/body/eval_jaxpr/psum | solution.py:16
  354.6 30.8 %all-reduce.5 = bf16[64,64]{1,0:T(8,128)(2,1)S(1)} all-reduce(bf16[64,64]{1,0:T(8,128)(2,1)S(1)} %convolution_convert_fusion.2), channel_id=2, replica_groups=mesh['blk'=64,'fld'=8] {'fld'}, use_global_device_ids=true, to_apply=%region_2.2.clone | all-reduce | flops 4096 | bytes 16384 | tf_op jit(solution)/shard_map/while
  385.3 1.3 dynamic-slice.6
  387.4 0.8 convert_dynamic-update-slice_fusion.5
  396.2 132.0 %all-reduce.4 = (bf16[2048]{0:T(1024)(128)(2,1)S(1)}, bf16[1]{0:T(256)(128)(2,1)}) all-reduce(bf16[2048]{0:T(1024)(128)(2,1)S(1)} %fusion.11, bf16[1]{0:T(256)(128)(2,1)} %bitcast.37), channel_id=1, replica_groups=mesh['blk'=64,'fld'=8] {'blk'}, use_global_device_ids=true, to_apply=%region_1.1 | all-reduce | flops 2049 | bytes 8196 | tf_op jit(solution)/shard_map/while/body/eval_jaxpr/psum | solution.py:16
  530.5 30.6 %all-reduce.5 = bf16[64,64]{1,0:T(8,128)(2,1)S(1)} all-reduce(bf16[64,64]{1,0:T(8,128)(2,1)S(1)} %convolution_convert_fusion.2), channel_id=2, replica_groups=mesh['blk'=64,'fld'=8] {'fld'}, use_global_device_ids=true, to_apply=%region_2.2.clone | all-reduce | flops 4096 | bytes 16384 | tf_op jit(solution)/shard_map/while
  561.1 1.3 dynamic-slice.6
  563.2 0.8 convert_dynamic-update-slice_fusion.5
  572.0 132.0 %all-reduce.4 = (bf16[2048]{0:T(1024)(128)(2,1)S(1)}, bf16[1]{0:T(256)(128)(2,1)}) all-reduce(bf16[2048]{0:T(1024)(128)(2,1)S(1)} %fusion.11, bf16[1]{0:T(256)(128)(2,1)} %bitcast.37), channel_id=1, replica_groups=mesh['blk'=64,'fld'=8] {'blk'}, use_global_device_ids=true, to_apply=%region_1.1 | all-reduce | flops 2049 | bytes 8196 | tf_op jit(solution)/shard_map/while/body/eval_jaxpr/psum | solution.py:16
  706.3 30.6 %all-reduce.5 = bf16[64,64]{1,0:T(8,128)(2,1)S(1)} all-reduce(bf16[64,64]{1,0:T(8,128)(2,1)S(1)} %convolution_convert_fusion.2), channel_id=2, replica_groups=mesh['blk'=64,'fld'=8] {'fld'}, use_global_device_ids=true, to_apply=%region_2.2.clone | all-reduce | flops 4096 | bytes 16384 | tf_op jit(solution)/shard_map/while
  737.0 1.3 dynamic-slice.6
  739.0 0.8 convert_dynamic-update-slice_fusion.5
  747.8 132.0 %all-reduce.4 = (bf16[2048]{0:T(1024)(128)(2,1)S(1)}, bf16[1]{0:T(256)(128)(2,1)}) all-reduce(bf16[2048]{0:T(1024)(128)(2,1)S(1)} %fusion.11, bf16[1]{0:T(256)(128)(2,1)} %bitcast.37), channel_id=1, replica_groups=mesh['blk'=64,'fld'=8] {'blk'}, use_global_device_ids=true, to_apply=%region_1.1 | all-reduce | flops 2049 | bytes 8196 | tf_op jit(solution)/shard_map/while/body/eval_jaxpr/psum | solution.py:16
  882.2 30.6 %all-reduce.5 = bf16[64,64]{1,0:T(8,128)(2,1)S(1)} all-reduce(bf16[64,64]{1,0:T(8,128)(2,1)S(1)} %convolution_convert_fusion.2), channel_id=2, replica_groups=mesh['blk'=64,'fld'=8] {'fld'}, use_global_device_ids=true, to_apply=%region_2.2.clone | all-reduce | flops 4096 | bytes 16384 | tf_op jit(solution)/shard_map/while
  912.8 1.3 dynamic-slice.6
  914.9 0.8 convert_dynamic-update-slice_fusion.5
  923.7 132.0 %all-reduce.4 = (bf16[2048]{0:T(1024)(128)(2,1)S(1)}, bf16[1]{0:T(256)(128)(2,1)}) all-reduce(bf16[2048]{0:T(1024)(128)(2,1)S(1)} %fusion.11, bf16[1]{0:T(256)(128)(2,1)} %bitcast.37), channel_id=1, replica_groups=mesh['blk'=64,'fld'=8] {'blk'}, use_global_device_ids=true, to_apply=%region_1.1 | all-reduce | flops 2049 | bytes 8196 | tf_op jit(solution)/shard_map/while/body/eval_jaxpr/psum | solution.py:16
  1058.0 30.6 %all-reduce.5 = bf16[64,64]{1,0:T(8,128)(2,1)S(1)} all-reduce(bf16[64,64]{1,0:T(8,128)(2,1)S(1)} %convolution_convert_fusion.2), channel_id=2, replica_groups=mesh['blk'=64,'fld'=8] {'fld'}, use_global_device_ids=true, to_apply=%region_2.2.clone | all-reduce | flops 4096 | bytes 16384 | tf_op jit(solution)/shard_map/while
  1088.6 1.3 dynamic-slice.6
  1099.5 132.0 %all-reduce.4 = (bf16[2048]{0:T(1024)(128)(2,1)S(1)}, bf16[1]{0:T(256)(128)(2,1)}) all-reduce(bf16[2048]{0:T(1024)(128)(2,1)S(1)} %fusion.11, bf16[1]{0:T(256)(128)(2,1)} %bitcast.37), channel_id=1, replica_groups=mesh['blk'=64,'fld'=8] {'blk'}, use_global_device_ids=true, to_apply=%region_1.1 | all-reduce | flops 2049 | bytes 8196 | tf_op jit(solution)/shard_map/while/body/eval_jaxpr/psum | solution.py:16
  1233.8 30.6 %all-reduce.5 = bf16[64,64]{1,0:T(8,128)(2,1)S(1)} all-reduce(bf16[64,64]{1,0:T(8,128)(2,1)S(1)} %convolution_convert_fusion.2), channel_id=2, replica_groups=mesh['blk'=64,'fld'=8] {'fld'}, use_global_device_ids=true, to_apply=%region_2.2.clone | all-reduce | flops 4096 | bytes 16384 | tf_op jit(solution)/shard_map/while
  1264.5 1.3 dynamic-slice.6
  (100 shorter events, 22.1 us)
Async XLA Ops:
  0.0 63.1 %copy-start = (bf16[64,2048]{1,0:T(8,128)(2,1)S(1)}, bf16[64,2048]{1,0:T(8,128)(2,1)}, u32[]{:S(2)}) copy-start(bf16[64,2048]{1,0:T(8,128)(2,1)} %param.7) | copy-start | bytes 786436
  0.0 22.6 %collective-permute-start.9 = (bf16[64]{0:T(256)(128)(2,1)}, bf16[64]{0:T(256)(128)(2,1)S(1)}, u32[]{:S(2)}, u32[]{:S(2)}) collective-permute-start(bf16[64]{0:T(256)(128)(2,1)} %param.8), channel_id=1, source_target_pairs={{0,504},{8,0},{16,8},{24,16},{32,24},{40,32},{48,40},{56,48},{64,5... | collective-permute-start | bytes 392 | tf_op jit(solution)/shard_map/ppermute | solution.py:11
  10.7 52.3 %collective-permute-start = (bf16[64,2048]{1,0:T(8,128)(2,1)}, bf16[64,2048]{1,0:T(8,128)(2,1)S(1)}, u32[]{:S(2)}, u32[]{:S(2)}) collective-permute-start(bf16[64,2048]{1,0:T(8,128)(2,1)} %param.7), channel_id=1, source_target_pairs={{0,504},{8,0},{16,8},{24,16},{32,24},{40,32},{48,40},{56,48},{64,5... | collective-permute-start | bytes 786440 | tf_op jit(solution)/shard_map/ppermute | solution.py:11
  20.4 0.7 copy-start.2
  21.2 0.7 copy-start.1
  21.8 0.7 copy-start.3
  22.6 5.8 collective-permute-start.10
  25.5 7.5 collective-permute-start.14
  28.5 8.0 collective-permute-start.11
  33.1 7.2 collective-permute-start.15
  36.5 9.4 collective-permute-start.12
  40.3 15.9 %collective-permute-start.16 = (bf16[64]{0:T(256)(128)(2,1)S(1)}, bf16[64]{0:T(256)(128)(2,1)S(1)}, u32[]{:S(2)}, u32[]{:S(2)}) collective-permute-start(bf16[64]{0:T(256)(128)(2,1)S(1)} %broadcast_select_fusion.11), channel_id=1, source_target_pairs={{0,448},{8,456},{16,464},{24,472},{32,480},{40,488},{48,496},{56,5... | collective-permute-start | bytes 392 | tf_op jit(solution)/shard_map/ppermute | solution.py:11
  45.8 17.2 %collective-permute-start.13 = (bf16[64]{0:T(256)(128)(2,1)S(1)}, bf16[64]{0:T(256)(128)(2,1)S(1)}, u32[]{:S(2)}, u32[]{:S(2)}) collective-permute-start(bf16[64]{0:T(256)(128)(2,1)S(1)} %broadcast_select_fusion.17), channel_id=1, source_target_pairs={{0,384},{8,392},{16,400},{24,408},{32,416},{40,424},{48,432},{56,4... | collective-permute-start | bytes 392 | tf_op jit(solution)/shard_map/ppermute | solution.py:11
  56.2 17.4 %collective-permute-start.17 = (bf16[64]{0:T(256)(128)(2,1)S(1)}, bf16[64]{0:T(256)(128)(2,1)S(1)}, u32[]{:S(2)}, u32[]{:S(2)}) collective-permute-start(bf16[64]{0:T(256)(128)(2,1)S(1)} %broadcast_select_fusion.12), channel_id=1, source_target_pairs={{0,384},{8,392},{16,400},{24,408},{32,416},{40,424},{48,432},{56,4... | collective-permute-start | bytes 392 | tf_op jit(solution)/shard_map/ppermute | solution.py:11
  63.2 17.8 %collective-permute-start.1 = (bf16[64,2048]{1,0:T(8,128)(2,1)S(1)}, bf16[64,2048]{1,0:T(8,128)(2,1)S(1)}, u32[]{:S(2)}, u32[]{:S(2)}) collective-permute-start(bf16[64,2048]{1,0:T(8,128)(2,1)S(1)} %get-tuple-element.142), channel_id=1, source_target_pairs={{0,496},{8,504},{16,0},{24,8},{32,16},{40,24},{48,32},{56,40},{64,... | collective-permute-start | bytes 786440 | tf_op jit(solution)/shard_map/ppermute | solution.py:11
  73.7 18.3 %collective-permute-start.5 = (bf16[64,2048]{1,0:T(8,128)(2,1)S(1)}, bf16[64,2048]{1,0:T(8,128)(2,1)S(1)}, u32[]{:S(2)}, u32[]{:S(2)}) collective-permute-start(bf16[64,2048]{1,0:T(8,128)(2,1)S(1)} %get-tuple-element.143), channel_id=1, source_target_pairs={{0,496},{8,504},{16,0},{24,8},{32,16},{40,24},{48,32},{56,40},{64,... | collective-permute-start | bytes 786440 | tf_op jit(solution)/shard_map/ppermute | solution.py:11
  81.0 20.5 %collective-permute-start.2 = (bf16[64,2048]{1,0:T(8,128)(2,1)S(1)}, bf16[64,2048]{1,0:T(8,128)(2,1)S(1)}, u32[]{:S(2)}, u32[]{:S(2)}) collective-permute-start(bf16[64,2048]{1,0:T(8,128)(2,1)S(1)} %broadcast_select_fusion.6), channel_id=1, source_target_pairs={{0,480},{8,488},{16,496},{24,504},{32,0},{40,8},{48,16},{56,24},{6... | collective-permute-start | bytes 786440 | tf_op jit(solution)/shard_map/ppermute | solution.py:11
  92.0 47.6 %collective-permute-start.6 = (bf16[64,2048]{1,0:T(8,128)(2,1)S(1)}, bf16[64,2048]{1,0:T(8,128)(2,1)S(1)}, u32[]{:S(2)}, u32[]{:S(2)}) collective-permute-start(bf16[64,2048]{1,0:T(8,128)(2,1)S(1)} %broadcast_select_fusion.2), channel_id=1, source_target_pairs={{0,480},{8,488},{16,496},{24,504},{32,0},{40,8},{48,16},{56,24},{6... | collective-permute-start | bytes 786440 | tf_op jit(solution)/shard_map/ppermute | solution.py:11
  101.5 61.5 %collective-permute-start.3 = (bf16[64,2048]{1,0:T(8,128)(2,1)S(1)}, bf16[64,2048]{1,0:T(8,128)(2,1)S(1)}, u32[]{:S(2)}, u32[]{:S(2)}) collective-permute-start(bf16[64,2048]{1,0:T(8,128)(2,1)S(1)} %broadcast_select_fusion.7), channel_id=1, source_target_pairs={{0,448},{8,456},{16,464},{24,472},{32,480},{40,488},{48,496},{56,5... | collective-permute-start | bytes 786440 | tf_op jit(solution)/shard_map/ppermute | solution.py:11
  139.6 52.8 %collective-permute-start.7 = (bf16[64,2048]{1,0:T(8,128)(2,1)S(1)}, bf16[64,2048]{1,0:T(8,128)(2,1)S(1)}, u32[]{:S(2)}, u32[]{:S(2)}) collective-permute-start(bf16[64,2048]{1,0:T(8,128)(2,1)S(1)} %broadcast_select_fusion.3), channel_id=1, source_target_pairs={{0,448},{8,456},{16,464},{24,472},{32,480},{40,488},{48,496},{56,5... | collective-permute-start | bytes 786440 | tf_op jit(solution)/shard_map/ppermute | solution.py:11
  163.1 35.0 %collective-permute-start.4 = (bf16[64,2048]{1,0:T(8,128)(2,1)S(1)}, bf16[64,2048]{1,0:T(8,128)(2,1)S(1)}, u32[]{:S(2)}, u32[]{:S(2)}) collective-permute-start(bf16[64,2048]{1,0:T(8,128)(2,1)S(1)} %broadcast_select_fusion.8), channel_id=1, source_target_pairs={{0,384},{8,392},{16,400},{24,408},{32,416},{40,424},{48,432},{56,4... | collective-permute-start | bytes 786440 | tf_op jit(solution)/shard_map/ppermute | solution.py:11
  192.5 19.6 %collective-permute-start.8 = (bf16[64,2048]{1,0:T(8,128)(2,1)S(1)}, bf16[64,2048]{1,0:T(8,128)(2,1)S(1)}, u32[]{:S(2)}, u32[]{:S(2)}) collective-permute-start(bf16[64,2048]{1,0:T(8,128)(2,1)S(1)} %broadcast_select_fusion.4), channel_id=1, source_target_pairs={{0,384},{8,392},{16,400},{24,408},{32,416},{40,424},{48,432},{56,4... | collective-permute-start | bytes 786440 | tf_op jit(solution)/shard_map/ppermute | solution.py:11
where the time goes:
time: 1270 us
  blocking collectives  976 us (77%)
  starting transfers between devices  130 us (10%)
  waiting for transfers between devices  72.3 us (6%)
  loops' own time  49.3 us (4%)
  local copies, waits for them, and re-layouts  27 us (2%)
    psum x6, blocking collectives, from_root(): return lax.psum(jnp.where(mine, value, jnp.zeros_like(value)), axis)  792 us
    while x6, blocking collectives  184 us
    ppermute x18, starting transfers between devices, from_behind(): lax.ppermute(value, axis, [(i, (i + by) % peers) for i in range(peers)])  130 us
    ppermute x18, waiting for transfers between devices, from_behind(): lax.ppermute(value, axis, [(i, (i + by) % peers) for i in range(peers)])  72.3 us
    another operation x1, loops' own time, body(): lax.scan(step_each, jnp.zeros((), jnp.float32), step_ids)  49.3 us
  transfers between devices with their start and end apart: 18, of which 6 were waited for; matrix products, arithmetic and copies ran while one was open for 0% of the time, Pallas kernels for 0%

commit v1 on v0

--- a/solution.py
+++ b/solution.py
@@ -13,7 +13,7 @@
 
 def from_root(value, axis, root):
     mine = lax.axis_index(axis) == root
-    return lax.psum(jnp.where(mine, value, jnp.zeros_like(value)), axis)
+    return jnp.sum(lax.all_gather(jnp.where(mine, value, jnp.zeros_like(value)), axis), axis=0)
 
 
 def body(vectors, norms, offsets, pivot_block, pivot_row):

time: 1270 us -> 1700 us (1.34)
  the two profiles are of different devices: /device:TPU:16 before, /device:TPU:48 now
where the time goes in v1:
time: 1700 us
  blocking collectives  1410 us (83%)
  starting transfers between devices  99.6 us (6%)
  waiting for transfers between devices  81.7 us (5%)
  loops' own time  45.7 us (3%)
  local copies, waits for them, and re-layouts  38.9 us (2%)
    while x12, blocking collectives  943 us
    all_gather x6, blocking collectives, from_root(): lax.all_gather(jnp.where(mine, value, jnp.zeros_like(value)), axis)  471 us
    ppermute x18, starting transfers between devices, from_behind(): lax.ppermute(value, axis, [(i, (i + by) % peers) for i in range(peers)])  99.6 us
    ppermute x18, waiting for transfers between devices, from_behind(): lax.ppermute(value, axis, [(i, (i + by) % peers) for i in range(peers)])  81.7 us
    another operation x1, loops' own time, body(): lax.scan(step_each, jnp.zeros((), jnp.float32), step_ids)  45.7 us
  transfers between devices with their start and end apart: 18, of which 9 were waited for; matrix products, arithmetic and copies ran while one was open for 0% of the time, Pallas kernels for 0%

profile of v1, /device:TPU:48, one launch (start us, length us, event | category | flops | bytes accessed | tf_op | source)
XLA Modules:
  0.0 1699.7 jit_solution(15468801070756908210)
XLA Ops:
  0.0 2.0 collective-permute-start.9
  2.1 2.1 collective-permute-start
  4.2 1.4 fusion.7
  12.9 11.2 collective-permute-start.10
  24.1 2.9 collective-permute-start.14
  27.0 6.6 collective-permute-start.11
  33.6 2.9 collective-permute-start.15
  36.6 3.1 collective-permute-start.12
  40.0 3.0 collective-permute-start.16
  43.1 2.9 collective-permute-done.12
  45.9 10.3 collective-permute-start.13
  56.3 6.8 collective-permute-start.17
  63.2 1.9 collective-permute-start.1
  65.2 5.3 collective-permute-done.17
  70.5 4.7 collective-permute-start.5
  75.3 10.3 collective-permute-start.2
  85.6 13.6 collective-permute-start.6
  99.9 3.8 collective-permute-start.3
  103.7 17.0 %collective-permute-done.6 = bf16[64,2048]{1,0:T(8,128)(2,1)S(1)} collective-permute-done((bf16[64,2048]{1,0:T(8,128)(2,1)S(1)}, bf16[64,2048]{1,0:T(8,128)(2,1)S(1)}, u32[]{:S(2)}, u32[]{:S(2)}) %collective-permute-start.6) | collective-permute-done | bytes 262176 | tf_op jit(solution)/shard_map/ppermute | solution.py:11
  120.8 1.9 collective-permute-start.7
  122.7 7.9 collective-permute-done.3
  130.7 6.0 collective-permute-start.4
  136.7 9.7 collective-permute-done.7
  146.4 6.5 collective-permute-start.8
  152.9 35.0 %collective-permute-done.4 = bf16[64,2048]{1,0:T(8,128)(2,1)S(1)} collective-permute-done((bf16[64,2048]{1,0:T(8,128)(2,1)S(1)}, bf16[64,2048]{1,0:T(8,128)(2,1)S(1)}, u32[]{:S(2)}, u32[]{:S(2)}) %collective-permute-start.4) | collective-permute-done | bytes 262176 | tf_op jit(solution)/shard_map/ppermute | solution.py:11
  187.9 2.8 collective-permute-done.8
  190.8 1508.1 %while.15 = (s32[]{:T(128)}, f32[6,8,64]{2,1,0:T(8,128)S(1)}, f32[6]{0:T(128)S(1)}, bf16[64,2048]{1,0:T(8,128)(2,1)S(1)}, s32[6]{0:T(128)S(1)}, /*index=5*/s32[6...) while((s32[]{:T(128)}, f32[6,8,64]{2,1,0:T(8,128)S(1)}, ...), condition=%wide.region_4.5_spmd, body=%wide.region_0.4_spmd.sunk | while | flops 17312408 | bytes 1117312 | solution.py:72
  200.3 1.3 dynamic-slice.8
  202.3 1.3 dynamic-slice.9
  204.3 144.0 %all-reduce.5 = bf16[64]{0:T(256)(128)(2,1)S(1)} all-reduce(bf16[64]{0:T(256)(128)(2,1)S(1)} %dynamic-update-slice.2), channel_id=1, replica_groups=mesh['blk'=64,'fld'=8] {'blk'}, use_global_device_ids=true, to_apply=%add | all-reduce | flops 64 | bytes 256 | tf_op jit(solution)/shard_map/while
  349.7 78.6 %all-gather.2 = bf16[64,1,2048]{2,1,0:T(2,128)(2,1)S(1)} all-gather(bf16[1,1,2048]{2,1,0:T(2,128)(2,1)S(1)} %fusion.11), channel_id=1, replica_groups=mesh['blk'=64,'fld'=8] {'blk'}, dimensions={0}, use_global_device_ids=true | all-gather | bytes 266240 | tf_op jit(solution)/shard_map/while/body/eval_jaxpr/all_gather | solution.py:16
  429.0 30.7 %all-reduce.4 = bf16[64,64]{1,0:T(8,128)(2,1)S(1)} all-reduce(bf16[64,64]{1,0:T(8,128)(2,1)S(1)} %convolution_convert_fusion.2), channel_id=2, replica_groups=mesh['blk'=64,'fld'=8] {'fld'}, use_global_device_ids=true, to_apply=%region_2.2.clone | all-reduce | flops 4096 | bytes 16384 | tf_op jit(solution)/shard_map/while
  473.2 123.0 %all-reduce.5 = bf16[64]{0:T(256)(128)(2,1)S(1)} all-reduce(bf16[64]{0:T(256)(128)(2,1)S(1)} %dynamic-update-slice.2), channel_id=1, replica_groups=mesh['blk'=64,'fld'=8] {'blk'}, use_global_device_ids=true, to_apply=%add | all-reduce | flops 64 | bytes 256 | tf_op jit(solution)/shard_map/while
  597.6 78.6 %all-gather.2 = bf16[64,1,2048]{2,1,0:T(2,128)(2,1)S(1)} all-gather(bf16[1,1,2048]{2,1,0:T(2,128)(2,1)S(1)} %fusion.11), channel_id=1, replica_groups=mesh['blk'=64,'fld'=8] {'blk'}, dimensions={0}, use_global_device_ids=true | all-gather | bytes 266240 | tf_op jit(solution)/shard_map/while/body/eval_jaxpr/all_gather | solution.py:16
  676.9 30.6 %all-reduce.4 = bf16[64,64]{1,0:T(8,128)(2,1)S(1)} all-reduce(bf16[64,64]{1,0:T(8,128)(2,1)S(1)} %convolution_convert_fusion.2), channel_id=2, replica_groups=mesh['blk'=64,'fld'=8] {'fld'}, use_global_device_ids=true, to_apply=%region_2.2.clone | all-reduce | flops 4096 | bytes 16384 | tf_op jit(solution)/shard_map/while
  717.0 1.3 dynamic-slice.8
  721.1 123.0 %all-reduce.5 = bf16[64]{0:T(256)(128)(2,1)S(1)} all-reduce(bf16[64]{0:T(256)(128)(2,1)S(1)} %dynamic-update-slice.2), channel_id=1, replica_groups=mesh['blk'=64,'fld'=8] {'blk'}, use_global_device_ids=true, to_apply=%add | all-reduce | flops 64 | bytes 256 | tf_op jit(solution)/shard_map/while
  845.5 78.6 %all-gather.2 = bf16[64,1,2048]{2,1,0:T(2,128)(2,1)S(1)} all-gather(bf16[1,1,2048]{2,1,0:T(2,128)(2,1)S(1)} %fusion.11), channel_id=1, replica_groups=mesh['blk'=64,'fld'=8] {'blk'}, dimensions={0}, use_global_device_ids=true | all-gather | bytes 266240 | tf_op jit(solution)/shard_map/while/body/eval_jaxpr/all_gather | solution.py:16
  924.7 30.6 %all-reduce.4 = bf16[64,64]{1,0:T(8,128)(2,1)S(1)} all-reduce(bf16[64,64]{1,0:T(8,128)(2,1)S(1)} %convolution_convert_fusion.2), channel_id=2, replica_groups=mesh['blk'=64,'fld'=8] {'fld'}, use_global_device_ids=true, to_apply=%region_2.2.clone | all-reduce | flops 4096 | bytes 16384 | tf_op jit(solution)/shard_map/while
  968.9 123.0 %all-reduce.5 = bf16[64]{0:T(256)(128)(2,1)S(1)} all-reduce(bf16[64]{0:T(256)(128)(2,1)S(1)} %dynamic-update-slice.2), channel_id=1, replica_groups=mesh['blk'=64,'fld'=8] {'blk'}, use_global_device_ids=true, to_apply=%add | all-reduce | flops 64 | bytes 256 | tf_op jit(solution)/shard_map/while
  1093.3 78.6 %all-gather.2 = bf16[64,1,2048]{2,1,0:T(2,128)(2,1)S(1)} all-gather(bf16[1,1,2048]{2,1,0:T(2,128)(2,1)S(1)} %fusion.11), channel_id=1, replica_groups=mesh['blk'=64,'fld'=8] {'blk'}, dimensions={0}, use_global_device_ids=true | all-gather | bytes 266240 | tf_op jit(solution)/shard_map/while/body/eval_jaxpr/all_gather | solution.py:16
  1172.6 30.6 %all-reduce.4 = bf16[64,64]{1,0:T(8,128)(2,1)S(1)} all-reduce(bf16[64,64]{1,0:T(8,128)(2,1)S(1)} %convolution_convert_fusion.2), channel_id=2, replica_groups=mesh['blk'=64,'fld'=8] {'fld'}, use_global_device_ids=true, to_apply=%region_2.2.clone | all-reduce | flops 4096 | bytes 16384 | tf_op jit(solution)/shard_map/while
  1216.7 123.0 %all-reduce.5 = bf16[64]{0:T(256)(128)(2,1)S(1)} all-reduce(bf16[64]{0:T(256)(128)(2,1)S(1)} %dynamic-update-slice.2), channel_id=1, replica_groups=mesh['blk'=64,'fld'=8] {'blk'}, use_global_device_ids=true, to_apply=%add | all-reduce | flops 64 | bytes 256 | tf_op jit(solution)/shard_map/while
  1341.2 78.6 %all-gather.2 = bf16[64,1,2048]{2,1,0:T(2,128)(2,1)S(1)} all-gather(bf16[1,1,2048]{2,1,0:T(2,128)(2,1)S(1)} %fusion.11), channel_id=1, replica_groups=mesh['blk'=64,'fld'=8] {'blk'}, dimensions={0}, use_global_device_ids=true | all-gather | bytes 266240 | tf_op jit(solution)/shard_map/while/body/eval_jaxpr/all_gather | solution.py:16
  1420.4 30.6 %all-reduce.4 = bf16[64,64]{1,0:T(8,128)(2,1)S(1)} all-reduce(bf16[64,64]{1,0:T(8,128)(2,1)S(1)} %convolution_convert_fusion.2), channel_id=2, replica_groups=mesh['blk'=64,'fld'=8] {'fld'}, use_global_device_ids=true, to_apply=%region_2.2.clone | all-reduce | flops 4096 | bytes 16384 | tf_op jit(solution)/shard_map/while
  1464.6 123.0 %all-reduce.5 = bf16[64]{0:T(256)(128)(2,1)S(1)} all-reduce(bf16[64]{0:T(256)(128)(2,1)S(1)} %dynamic-update-slice.2), channel_id=1, replica_groups=mesh['blk'=64,'fld'=8] {'blk'}, use_global_device_ids=true, to_apply=%add | all-reduce | flops 64 | bytes 256 | tf_op jit(solution)/shard_map/while
  1589.0 78.6 %all-gather.2 = bf16[64,1,2048]{2,1,0:T(2,128)(2,1)S(1)} all-gather(bf16[1,1,2048]{2,1,0:T(2,128)(2,1)S(1)} %fusion.11), channel_id=1, replica_groups=mesh['blk'=64,'fld'=8] {'blk'}, dimensions={0}, use_global_device_ids=true | all-gather | bytes 266240 | tf_op jit(solution)/shard_map/while/body/eval_jaxpr/all_gather | solution.py:16
  1668.3 30.6 %all-reduce.4 = bf16[64,64]{1,0:T(8,128)(2,1)S(1)} all-reduce(bf16[64,64]{1,0:T(8,128)(2,1)S(1)} %convolution_convert_fusion.2), channel_id=2, replica_groups=mesh['blk'=64,'fld'=8] {'fld'}, use_global_device_ids=true, to_apply=%region_2.2.clone | all-reduce | flops 4096 | bytes 16384 | tf_op jit(solution)/shard_map/while
  (136 shorter events, 48.3 us)
Async XLA Ops:
  0.0 63.2 %copy-start = (bf16[64,2048]{1,0:T(8,128)(2,1)S(1)}, bf16[64,2048]{1,0:T(8,128)(2,1)}, u32[]{:S(2)}) copy-start(bf16[64,2048]{1,0:T(8,128)(2,1)} %param.7) | copy-start | bytes 786436
  0.0 12.9 collective-permute-start.9
  2.1 61.1 %collective-permute-start = (bf16[64,2048]{1,0:T(8,128)(2,1)}, bf16[64,2048]{1,0:T(8,128)(2,1)S(1)}, u32[]{:S(2)}, u32[]{:S(2)}) collective-permute-start(bf16[64,2048]{1,0:T(8,128)(2,1)} %param.7), channel_id=1, source_target_pairs={{0,504},{8,0},{16,8},{24,16},{32,24},{40,32},{48,40},{56,48},{64,5... | collective-permute-start | bytes 786440 | tf_op jit(solution)/shard_map/ppermute | solution.py:11
  10.8 0.7 copy-start.1
  11.5 0.7 copy-start.2
  12.1 0.7 copy-start.3
  12.9 14.1 collective-permute-start.10
  24.1 9.5 collective-permute-start.14
  27.0 9.5 collective-permute-start.11
  33.6 6.4 collective-permute-start.15
  36.6 9.4 collective-permute-start.12
  40.0 16.3 collective-permute-start.16
  45.9 17.2 %collective-permute-start.13 = (bf16[64]{0:T(256)(128)(2,1)S(1)}, bf16[64]{0:T(256)(128)(2,1)S(1)}, u32[]{:S(2)}, u32[]{:S(2)}) collective-permute-start(bf16[64]{0:T(256)(128)(2,1)S(1)} %broadcast_select_fusion.17), channel_id=1, source_target_pairs={{0,384},{8,392},{16,400},{24,408},{32,416},{40,424},{48,432},{56,4... | collective-permute-start | bytes 392 | tf_op jit(solution)/shard_map/ppermute | solution.py:11
  56.3 14.2 collective-permute-start.17
  63.2 12.0 collective-permute-start.1
  70.5 15.0 collective-permute-start.5
  75.3 24.6 %collective-permute-start.2 = (bf16[64,2048]{1,0:T(8,128)(2,1)S(1)}, bf16[64,2048]{1,0:T(8,128)(2,1)S(1)}, u32[]{:S(2)}, u32[]{:S(2)}) collective-permute-start(bf16[64,2048]{1,0:T(8,128)(2,1)S(1)} %broadcast_select_fusion.6), channel_id=1, source_target_pairs={{0,480},{8,488},{16,496},{24,504},{32,0},{40,8},{48,16},{56,24},{6... | collective-permute-start | bytes 786440 | tf_op jit(solution)/shard_map/ppermute | solution.py:11
  85.6 35.2 %collective-permute-start.6 = (bf16[64,2048]{1,0:T(8,128)(2,1)S(1)}, bf16[64,2048]{1,0:T(8,128)(2,1)S(1)}, u32[]{:S(2)}, u32[]{:S(2)}) collective-permute-start(bf16[64,2048]{1,0:T(8,128)(2,1)S(1)} %broadcast_select_fusion.2), channel_id=1, source_target_pairs={{0,480},{8,488},{16,496},{24,504},{32,0},{40,8},{48,16},{56,24},{6... | collective-permute-start | bytes 786440 | tf_op jit(solution)/shard_map/ppermute | solution.py:11
  99.9 30.7 %collective-permute-start.3 = (bf16[64,2048]{1,0:T(8,128)(2,1)S(1)}, bf16[64,2048]{1,0:T(8,128)(2,1)S(1)}, u32[]{:S(2)}, u32[]{:S(2)}) collective-permute-start(bf16[64,2048]{1,0:T(8,128)(2,1)S(1)} %broadcast_select_fusion.7), channel_id=1, source_target_pairs={{0,448},{8,456},{16,464},{24,472},{32,480},{40,488},{48,496},{56,5... | collective-permute-start | bytes 786440 | tf_op jit(solution)/shard_map/ppermute | solution.py:11
  120.8 25.6 %collective-permute-start.7 = (bf16[64,2048]{1,0:T(8,128)(2,1)S(1)}, bf16[64,2048]{1,0:T(8,128)(2,1)S(1)}, u32[]{:S(2)}, u32[]{:S(2)}) collective-permute-start(bf16[64,2048]{1,0:T(8,128)(2,1)S(1)} %broadcast_select_fusion.3), channel_id=1, source_target_pairs={{0,448},{8,456},{16,464},{24,472},{32,480},{40,488},{48,496},{56,5... | collective-permute-start | bytes 786440 | tf_op jit(solution)/shard_map/ppermute | solution.py:11
  130.7 57.2 %collective-permute-start.4 = (bf16[64,2048]{1,0:T(8,128)(2,1)S(1)}, bf16[64,2048]{1,0:T(8,128)(2,1)S(1)}, u32[]{:S(2)}, u32[]{:S(2)}) collective-permute-start(bf16[64,2048]{1,0:T(8,128)(2,1)S(1)} %broadcast_select_fusion.8), channel_id=1, source_target_pairs={{0,384},{8,392},{16,400},{24,408},{32,416},{40,424},{48,432},{56,4... | collective-permute-start | bytes 786440 | tf_op jit(solution)/shard_map/ppermute | solution.py:11
  146.4 44.3 %collective-permute-start.8 = (bf16[64,2048]{1,0:T(8,128)(2,1)S(1)}, bf16[64,2048]{1,0:T(8,128)(2,1)S(1)}, u32[]{:S(2)}, u32[]{:S(2)}) collective-permute-start(bf16[64,2048]{1,0:T(8,128)(2,1)S(1)} %broadcast_select_fusion.4), channel_id=1, source_target_pairs={{0,384},{8,392},{16,400},{24,408},{32,416},{40,424},{48,432},{56,4... | collective-permute-start | bytes 786440 | tf_op jit(solution)/shard_map/ppermute | solution.py:11
